TPU v7x, 32 devices: a whole 2x2x4 slice. The times are simulated.
32 devices in a mesh: req: 2 (over x), ctx: 4 (over y, core), tp: 4 (over z).
Axes of the slice: x: 2, y: 2, z: 4, core: 2. Of those that a mesh axis runs over, the one named last changes fastest.
Arguments:
- queries: bfloat16 [512, 16, 128], P('req', 'tp'), may hold values from -5 to 5
- new_keys: bfloat16 [512, 4, 128], P('req', 'tp'), may hold values from -5 to 5
- new_values: bfloat16 [512, 4, 128], P('req', 'tp'), may hold values from -24 to 24
- cache_keys: bfloat16 [2, 8192, 4, 128], P('req', 'ctx', 'tp'), may hold values from -5 to 5
- cache_values: bfloat16 [2, 8192, 4, 128], P('req', 'ctx', 'tp'), may hold values from -24 to 24
- cache_lengths: int32 [2], replicated, may hold values from 1 to 8192, as said below
- residual: bfloat16 [512, 2048], P(('req', 'ctx'), 'tp'), may hold values from -24 to 24
- out_weight: bfloat16 [2048, 2048], P('tp', 'ctx'), may hold values from -0.52734375 to 0.52734375
- norm_gain: float32 [2048], replicated, may hold values from 0.1 to 1.9
- expert_ids: int32 [512, 6], P(('req', 'ctx')), may hold values from 0 to 63, all different within a row; in each aligned block of 64 rows (0 to 63, 64 to 127, ...) at most 8 rows name the same one
- gate_weights: float32 [512, 6], P(('req', 'ctx')), may hold values from 0.1 to 1
- w_gate: bfloat16 [64, 2048, 1408], P('req', 'ctx', 'tp'), may hold values from -0.125 to 0.125
- w_up: bfloat16 [64, 2048, 1408], P('req', 'ctx', 'tp'), may hold values from -0.125 to 0.125
- w_down: bfloat16 [64, 1408, 2048], P('req', 'tp', 'ctx'), may hold values from -0.15625 to 0.15625
Outputs:
- layer_out: bfloat16 [512, 2048], P(('req', 'ctx'), 'tp')
Inputs may be any that keep to these rules, and one draw needn't show every extreme that they name: `cache_lengths`: the longest cached length equals 8192. `expert_ids`: within each aligned block of 64 tokens no expert is named by more than 8 routes, a bound that some block reaches.
All inputs are finite; a program needn't handle non-finite values.
Results may differ from a plain program's by a relative error of at most 0.006.
Values may be sent and summed in bfloat16 or wider, within the bound.
A program may use at most 384 MiB of HBM per device.

v0:
```python
import jax
import jax.numpy as jnp
from jax import lax
from jax.sharding import PartitionSpec as P

TOP = 6
CAP = 8
MASKED = -1e30


def attention_part(queries, new_keys, new_values, cache_keys, cache_values, length):
    ctx_pos, ctx_count = (lax.axis_index("ctx"), lax.axis_size("ctx"))
    tok_dev, heads, hd = queries.shape
    cache_dev = cache_keys.shape[1]
    block = tok_dev // ctx_count
    rows = heads * block
    q = queries.reshape(ctx_count, block, heads, hd).transpose(0, 2, 1, 3)
    q = q.reshape(ctx_count * rows, hd)
    keys = jnp.concatenate([cache_keys[0, :, 0, :], new_keys[:, 0, :]], 0)
    values = jnp.concatenate([cache_values[0, :, 0, :], new_values[:, 0, :]], 0)
    scores = jnp.dot(keys, q.T, preferred_element_type=jnp.float32) * hd ** (-0.5)
    key_at = jnp.arange(cache_dev + tok_dev, dtype=jnp.int32)[:, None]
    row_at = jnp.arange(ctx_count * rows, dtype=jnp.int32)[None, :]
    token = row_at // rows * block + row_at % block
    valid = jnp.where(
        key_at < cache_dev,
        ctx_pos * cache_dev + key_at < length,
        jnp.logical_and(ctx_pos == ctx_count - 1, key_at - cache_dev <= token),
    )
    scores = jnp.where(valid, scores, MASKED)
    top = jnp.max(scores, 0, keepdims=True)
    weights = jnp.where(valid, jnp.exp(scores - top), 0.0)
    total = jnp.sum(weights, 0, keepdims=True)
    sums = lax.dot_general(
        values,
        weights.astype(jnp.bfloat16),
        (((0,), (0,)), ((), ())),
        preferred_element_type=jnp.float32,
    )
    pack = jnp.concatenate([sums, top, total, jnp.zeros((6, ctx_count * rows), jnp.float32)], 0)
    return pack.reshape(hd + 8, ctx_count, rows).transpose(1, 0, 2)


def merge(packs, hd, heads):
    top = jnp.max(packs[:, hd : hd + 1], 0)
    factor = jnp.exp(packs[:, hd : hd + 1] - top)
    total = jnp.sum(factor * packs[:, hd + 1 : hd + 2], 0)
    out = (jnp.sum(factor * packs[:, :hd], 0) / total).astype(jnp.bfloat16)
    block = out.shape[1] // heads
    return out.reshape(hd, heads, block).transpose(2, 1, 0).reshape(block, heads * hd)


def route_tables(expert_ids, gate_weights, exp_dev):
    block = expert_ids.shape[0]
    both = jnp.concatenate([expert_ids.astype(jnp.float32), gate_weights], 1)
    both = lax.all_gather(both, ("req", "ctx"))
    blocks = both.shape[0]
    ids = both[:, :, :TOP].astype(jnp.int32)
    gates = both[:, :, TOP:]
    first = lax.axis_index("req") * exp_dev
    experts = first + jnp.arange(exp_dev, dtype=jnp.int32)
    hits = ids[:, :, :, None] == experts
    gate_at = jnp.sum(jnp.where(hits, gates[..., None], 0.0), 2)
    hit = jnp.any(hits, 2)
    earlier = jnp.tril(jnp.ones((block, block), jnp.bfloat16), -1)
    rank = jnp.einsum(
        "ij,bje->bie", earlier, hit.astype(jnp.bfloat16), preferred_element_type=jnp.float32
    )
    code = jnp.arange(blocks, dtype=jnp.int32)[:, None, None] * CAP + rank.astype(jnp.int32)
    code = jnp.where(hit, code, -1)
    flat = (blocks * block, exp_dev)
    return (code.reshape(flat).T, gate_at.reshape(flat).T)


def body(
    queries,
    new_keys,
    new_values,
    cache_keys,
    cache_values,
    cache_lengths,
    residual,
    out_weight,
    norm_gain,
    expert_ids,
    gate_weights,
    w_gate,
    w_up,
    w_down,
):
    ctx_pos, tp_pos, req_pos = (lax.axis_index(a) for a in ("ctx", "tp", "req"))
    ctx_count, req_count = (lax.axis_size("ctx"), lax.axis_size("req"))
    tok_dev, heads, hd = queries.shape
    block, share = residual.shape
    exp_dev = w_gate.shape[0]
    slots = req_count * ctx_count * CAP
    length = lax.dynamic_index_in_dim(cache_lengths, req_pos, 0, keepdims=False)
    code, gate_at = route_tables(expert_ids, gate_weights, exp_dev)
    swap = [
        (a * ctx_count + b, b * ctx_count + a) for a in range(ctx_count) for b in range(ctx_count)
    ]
    residual_t = lax.ppermute(residual, ("ctx", "tp"), swap)
    packs = attention_part(queries, new_keys, new_values, cache_keys, cache_values, length)
    packs = lax.all_to_all(packs, "ctx", 0, 0, tiled=True)
    attended = merge(packs, hd, heads)
    attended = lax.all_gather(attended, "ctx", tiled=True)
    part = jnp.dot(attended, out_weight, preferred_element_type=jnp.float32)
    part = part.reshape(-1, block, share)
    part = lax.all_to_all(part, "tp", 0, 0, tiled=True)
    hidden = jnp.sum(part, 0) + residual_t.astype(jnp.float32)
    squares = jnp.sum(hidden * hidden, 1)
    gain = lax.dynamic_slice_in_dim(norm_gain, ctx_pos * share, share, 0)
    scaled = (hidden * gain).astype(jnp.bfloat16)
    squares = lax.psum(squares, "ctx")
    factor = lax.rsqrt(squares / norm_gain.shape[0] + 1e-06)
    factor = lax.all_gather(factor, ("req", "tp"), tiled=True)
    scaled = lax.all_gather(scaled, ("req", "tp"), tiled=True)
    pick = code[:, None, :] == jnp.arange(slots, dtype=jnp.int32)[None, :, None]
    row_factor = jnp.sum(jnp.where(pick, factor, 0.0), -1, keepdims=True)
    row_gate = jnp.sum(jnp.where(pick, gate_at[:, None, :], 0.0), -1, keepdims=True)
    pick = pick.astype(jnp.bfloat16)
    rows = jnp.einsum("est,td->esd", pick, scaled, preferred_element_type=jnp.bfloat16)
    gate = jnp.einsum("esd,edf->esf", rows, w_gate, preferred_element_type=jnp.float32)
    up = jnp.einsum("esd,edf->esf", rows, w_up, preferred_element_type=jnp.float32)
    both = jnp.stack([gate, up], 2).astype(jnp.bfloat16)
    both = both.reshape(ctx_count, exp_dev * slots // ctx_count, 2, -1)
    both = lax.all_to_all(both, "ctx", 0, 0, tiled=True)
    both = both.astype(jnp.float32).sum(0)
    per = exp_dev * slots // ctx_count
    mine = lax.dynamic_slice_in_dim(row_factor.reshape(-1, 1), ctx_pos * per, per, 0)
    inner = (jax.nn.silu(both[:, 0] * mine) * (both[:, 1] * mine)).astype(jnp.bfloat16)
    inner = lax.all_gather(inner, "ctx", tiled=True).reshape(exp_dev, slots, -1)
    down = jnp.einsum("esf,efd->esd", inner, w_down, preferred_element_type=jnp.float32)
    down = (down * row_gate).astype(jnp.bfloat16)
    mixed = jnp.einsum("est,esd->td", pick, down, preferred_element_type=jnp.float32)
    mixed = mixed.astype(jnp.bfloat16).reshape(-1, block, share)
    mixed = lax.all_to_all(mixed, ("req", "tp"), 0, 0, tiled=True)
    out = hidden + jnp.sum(mixed.astype(jnp.float32), 0)
    return lax.ppermute(out.astype(jnp.bfloat16), ("ctx", "tp"), swap)


def solution(mesh):
    in_specs = (
        P("req", "tp", None),
        P("req", "tp", None),
        P("req", "tp", None),
        P("req", "ctx", "tp", None),
        P("req", "ctx", "tp", None),
        P(),
        P(("req", "ctx"), "tp"),
        P("tp", "ctx"),
        P(),
        P(("req", "ctx"), None),
        P(("req", "ctx"), None),
        P("req", "ctx", "tp"),
        P("req", "ctx", "tp"),
        P("req", "tp", "ctx"),
    )
    out_specs = P(("req", "ctx"), "tp")
    return jax.shard_map(body, mesh=mesh, in_specs=in_specs, out_specs=out_specs, check_vma=False)
```

profile of v0, /device:TPU:4, one launch (start us, length us, event | category | flops | bytes accessed | tf_op | source)
XLA Modules:
  0.0 254.7 jit_solution(7631431469196999747)
XLA Ops:
  6.6 1.0 copy.55
  7.6 1.2 dynamic_slice.10
  8.9 0.7 add_compare_fusion
  9.5 6.5 %fusion = (f32[1024]{0:T(1024)S(1)}, f32[2304,1024]{1,0:T(8,128)S(1)}) fusion(s32[1024]{0:T(1024)S(1)} %fusion.38, s32[2304]{0:T(1024)S(1)} %iota_add_fusion, pred[2304]{0:T(1024)(128)(4,1)S(1)} %get-tuple-element.17, pred[2304]{0:T(1024)(128)(4,1)S(1)} %get-tuple-element.18, pred[]{:T(512)S(6)} %eq.16, bf16[1024,128]{1,0:T(8,128)(2,1)S(1)} %bitcast.83, ...), kind=kOutput, calls=%fused_computation.3 | convolution fusion | flops 619314176 | bytes 10311169 | tf_op jit(solution)/shard_map/dot_general | solution.py:21
  16.0 4.7 %fusion.1 = f32[1024]{0:T(1024)S(1)} fusion(f32[2304,1024]{1,0:T(8,128)S(1)} %get-tuple-element.16, f32[1024]{0:T(1024)S(1)} %get-tuple-element.15, s32[1024]{0:T(1024)S(1)} %fusion.38, s32[2304]{0:T(1024)S(1)} %iota_add_fusion, pred[2304]{0:T(1024)(128)(4,1)S(1)} %get-tuple-element.17, pred[2304]{0:T(1024)(128)(4,1)S(1)} %get-tuple-element.18, pred[]{:T(512)S(6)} %eq.16), kind=kLoop, calls=%fused_computation.5 | loop fusion | flops 18873344 | bytes 9463297 | tf_op jit(solution)/shard_map/reduce_sum | solution.py:33
  20.8 4.0 %fusion.3 = f32[128,1024]{1,0:T(8,128)S(1)} fusion(f32[2304,1024]{1,0:T(8,128)S(1)} %get-tuple-element.16, f32[1024]{0:T(1024)S(1)} %get-tuple-element.15, s32[1024]{0:T(1024)S(1)} %fusion.38, s32[2304]{0:T(1024)S(1)} %iota_add_fusion, pred[2304]{0:T(1024)(128)(4,1)S(1)} %get-tuple-element.17, pred[2304]{0:T(1024)(128)(4,1)S(1)} %get-tuple-element.18, ...), kind=kOutput, calls=%fused_computation.7 | convolution fusion | flops 624033792 | bytes 10573313 | tf_op jit(solution)/shard_map/dot_general | solution.py:34
  25.0 0.9 maximum_bitcast_fusion
  25.9 3.5 %all-to-all-start = ((f32[4,136,256]{2,1,0:T(8,128)}), f32[4,136,256]{2,1,0:T(8,128)S(1)}, u32[]{:S(2)}, u32[]{:S(2)}) async-start(f32[4,136,256]{2,1,0:T(8,128)} %maximum_bitcast_fusion), calls=%async_computation | async-start | bytes 1114112 | tf_op jit(solution)/shard_map/all_to_all | solution.py:104
  29.4 4.4 %collective-permute-start = (bf16[64,512]{1,0:T(8,128)(2,1)S(1)}, bf16[64,512]{1,0:T(8,128)(2,1)S(1)}, u32[]{:S(2)}, u32[]{:S(2)}) collective-permute-start(bf16[64,512]{1,0:T(8,128)(2,1)S(1)} %copy-done.14), channel_id=1, source_target_pairs={{0,0},{1,4},{2,8},{3,12},{4,1},{5,5},{6,9},{7,13},{8,2},{9,6},{10,... | collective-permute-start | bytes 196616 | tf_op jit(solution)/shard_map/ppermute | solution.py:102
  33.9 9.2 %all-gather.1 = f32[8,64,12]{1,2,0:T(8,128)S(1)} all-gather(f32[1,64,12]{1,2,0:T(8,128)S(1)} %maximum_bitcast_fusion.1), channel_id=2, replica_groups=mesh['req'=2,'ctx'=4,'tp'=4] {'req','ctx'}, dimensions={0}, use_global_device_ids=true | all-gather | bytes 27648 | tf_op jit(solution)/shard_map/all_gather | solution.py:56
  43.5 5.8 %all_gather.18 = bf16[256,512]{1,0:T(8,128)(2,1)S(1)} all-gather(bf16[64,512]{1,0:T(8,128)(2,1)S(1)} %copy_bitcast_fusion.1), channel_id=1, replica_groups=mesh['req'=2,'ctx'=4,'tp'=4] {'ctx'}, dimensions={0}, use_global_device_ids=true | all-gather | bytes 327680 | tf_op jit(solution)/shard_map/all_gather | solution.py:106
  49.4 1.1 fusion.53
  50.5 5.1 %all-to-all-start.1 = ((f32[4,64,512]{2,1,0:T(8,128)}), f32[4,64,512]{2,1,0:T(8,128)S(1)}, u32[]{:S(2)}, u32[]{:S(2)}) async-start(f32[4,64,512]{2,1,0:T(8,128)} %bitcast.13), calls=%async_computation.1 | async-start | bytes 1048576 | tf_op jit(solution)/shard_map/all_to_all | solution.py:109
  57.4 0.8 dynamic_slice.11
  58.2 12.4 %all-to-all-done.1 = f32[4,64,512]{2,1,0:T(8,128)S(1)} async-done(((f32[4,64,512]{2,1,0:T(8,128)}), f32[4,64,512]{2,1,0:T(8,128)S(1)}, u32[]{:S(2)}, u32[]{:S(2)}) %all-to-all-start.1) | async-done | bytes 524320 | tf_op jit(solution)/shard_map/all_to_all | solution.py:109
  70.8 32.5 %all_gather.21 = bf16[512,512]{1,0:T(8,128)(2,1)S(1)} all-gather(bf16[64,512]{1,0:T(8,128)(2,1)S(1)} %get-tuple-element.12), channel_id=1, replica_groups=mesh['req'=2,'ctx'=4,'tp'=4] {'req','tp'}, dimensions={0}, use_global_device_ids=true | all-gather | bytes 589824 | tf_op jit(solution)/shard_map/all_gather | solution.py:117
  103.3 1.3 fusion.6
  104.6 8.6 %convolution_convert_fusion = bf16[32,64,352]{2,1,0:T(8,128)(2,1)} fusion(bf16[32,64,512]{2,1,0:T(8,128)(2,1)S(1)} %fusion.6, bf16[32,512,352]{1,2,0:T(8,128)(2,1)} %param.26), kind=kOutput, calls=%fused_computation.17 | convolution fusion | flops 738918400 | bytes 15073280 | tf_op jit(solution)/shard_map/esd,edf->esf/dot_general | solution.py:124
  113.2 2.5 copy.63
  115.7 8.6 %convolution_convert_fusion.1 = bf16[32,64,352]{2,1,0:T(8,128)(2,1)} fusion(bf16[32,64,512]{2,1,0:T(8,128)(2,1)S(1)} %fusion.6, bf16[32,512,352]{1,2,0:T(8,128)(2,1)} %param.25), kind=kOutput, calls=%fused_computation.18 | convolution fusion | flops 738918400 | bytes 15073280 | tf_op jit(solution)/shard_map/esd,edf->esf/dot_general | solution.py:123
  124.3 1.7 copy.62
  126.0 3.2 %pad_maximum_fusion = bf16[4,512,2,352]{1,3,2,0:T(8,128)(2,1)} fusion(bf16[4,512,1,352]{1,3,2,0:T(8,128)(2,1)} %copy.63, bf16[4,512,1,352]{1,3,2,0:T(8,128)(2,1)S(1)} %copy.62), kind=kLoop, calls=%fused_computation.14 | loop fusion | flops 1441792 | bytes 5767168 | tf_op jit(solution)/shard_map/stack | solution.py:125
  129.3 5.4 %all-to-all-start.2 = ((bf16[4,512,2,352]{1,3,2,0:T(8,128)(2,1)}), bf16[4,512,2,352]{1,3,2,0:T(8,128)(2,1)S(1)}, u32[]{:S(2)}, u32[]{:S(2)}) async-start(bf16[4,512,2,352]{1,3,2,0:T(8,128)(2,1)} %pad_maximum_fusion), calls=%async_computation.2 | async-start | bytes 5767168 | tf_op jit(solution)/shard_map/all_to_all | solution.py:127
  136.3 33.5 %psum.7 = f32[64]{0:T(128)S(1)} all-reduce(f32[64]{0:T(128)S(1)} %get-tuple-element.11), channel_id=1, replica_groups=mesh['req'=2,'ctx'=4,'tp'=4] {'ctx'}, use_global_device_ids=true, to_apply=%region_9.10 | all-reduce | flops 64 | bytes 512 | tf_op jit(solution)/shard_map/psum | solution.py:114
  169.9 18.9 %all-reduce = f32[512]{0:T(512)S(1)} all-reduce(f32[512]{0:T(512)S(1)} %rsqrt_dynamic-update-slice_fusion), channel_id=1, replica_groups=mesh['req'=2,'ctx'=4,'tp'=4] {'req','tp'}, use_global_device_ids=true, to_apply=%add | all-reduce | flops 512 | bytes 4096
  188.8 1.5 select_reduce_fusion
  191.5 1.0 fusion.16
  192.5 17.0 %all-gather.4.cloned.1.call-done = bf16[2048,352]{1,0:T(8,128)(2,1)} async-done(((bf16[512,352]{1,0:T(8,128)(2,1)}), bf16[2048,352]{1,0:T(8,128)(2,1)}) %all-gather.4.cloned.1.call-update) | async-done | bytes 1441808 | tf_op jit(solution)/shard_map/all_gather | solution.py:132
  209.5 8.2 %fusion.10 = bf16[512,512]{1,0:T(8,128)(2,1)S(1)} fusion(s32[32,512]{1,0:T(8,128)S(1)} %bitcast.86, bf16[32,64,352]{2,1,0:T(8,128)(2,1)} %bitcast.92, bf16[32,352,512]{2,1,0:T(8,128)(2,1)} %param.27, f32[32,64]{1,0:T(8,128)S(1)} %get-tuple-element.5), kind=kOutput, calls=%fused_computation.20 | convolution fusion | flops 1815347200 | bytes 13574144 | tf_op jit(solution)/shard_map/est,esd->td/dot_general | solution.py:135
  217.8 21.4 %all_to_all.20 = bf16[8,64,512]{2,1,0:T(8,128)(2,1)S(1)} all-to-all(bf16[8,64,512]{2,1,0:T(8,128)(2,1)S(1)} %bitcast.81), channel_id=1, replica_groups=mesh['req'=2,'ctx'=4,'tp'=4] {'req','tp'}, dimensions={0} | all-to-all | bytes 1048576 | tf_op jit(solution)/shard_map/all_to_all | solution.py:137
  239.2 2.7 %collective-permute-start.1 = (bf16[64,512]{1,0:T(8,128)(2,1)S(1)}, bf16[64,512]{1,0:T(8,128)(2,1)S(1)}, u32[]{:S(2)}, u32[]{:S(2)}) collective-permute-start(bf16[64,512]{1,0:T(8,128)(2,1)S(1)} %add_convert_fusion), channel_id=1, source_target_pairs={{0,0},{1,4},{2,8},{3,12},{4,1},{5,5},{6,9},{7,13},{8,2},{9,6},{10,... | collective-permute-start | bytes 196616 | tf_op jit(solution)/shard_map/ppermute | solution.py:139
  242.0 5.2 %collective-permute-done.1 = bf16[64,512]{1,0:T(8,128)(2,1)S(1)} collective-permute-done((bf16[64,512]{1,0:T(8,128)(2,1)S(1)}, bf16[64,512]{1,0:T(8,128)(2,1)S(1)}, u32[]{:S(2)}, u32[]{:S(2)}) %collective-permute-start.1) | collective-permute-done | bytes 65568 | tf_op jit(solution)/shard_map/ppermute | solution.py:139
  (77 shorter events, 5.6 us)
Async XLA Ops:
  6.5 42.9 %copy-start = (bf16[512,512]{1,0:T(8,128)(2,1)S(1)}, bf16[512,512]{1,0:T(8,128)(2,1)}, u32[]{:S(2)}) copy-start(bf16[512,512]{1,0:T(8,128)(2,1)} %param.21) | copy-start | bytes 1572868
  16.0 4.8 %copy-start.12 = (bf16[1,2048,1,128]{3,1,2,0:T(8,128)(2,1)S(1)}, bf16[1,2048,1,128]{3,1,2,0:T(8,128)(2,1)}, u32[]{:S(2)}) copy-start(bf16[1,2048,1,128]{3,1,2,0:T(8,128)(2,1)} %param.18) | copy-start | bytes 1572868
  16.0 4.8 %copy-start.13 = (bf16[256,1,128]{2,0,1:T(8,128)(2,1)S(1)}, bf16[256,1,128]{2,0,1:T(8,128)(2,1)}, u32[]{:S(2)}) copy-start(bf16[256,1,128]{2,0,1:T(8,128)(2,1)} %param.16) | copy-start | bytes 196612
  20.8 8.6 %copy-start.14 = (bf16[64,512]{1,0:T(8,128)(2,1)S(1)}, bf16[64,512]{1,0:T(8,128)(2,1)}, u32[]{:S(2)}) copy-start(bf16[64,512]{1,0:T(8,128)(2,1)} %param.20) | copy-start | bytes 196612
  20.8 13.0 %copy-start.10 = (s32[64,6]{0,1:T(8,128)S(1)}, s32[64,6]{0,1:T(8,128)}, u32[]{:S(2)}) copy-start(s32[64,6]{0,1:T(8,128)} %param.23) | copy-start | bytes 4612
  20.8 13.1 %copy-start.11 = (f32[64,6]{0,1:T(8,128)S(1)}, f32[64,6]{0,1:T(8,128)}, u32[]{:S(2)}) copy-start(f32[64,6]{0,1:T(8,128)} %param.24) | copy-start | bytes 4612
  25.9 17.2 %all-to-all-start = ((f32[4,136,256]{2,1,0:T(8,128)}), f32[4,136,256]{2,1,0:T(8,128)S(1)}, u32[]{:S(2)}, u32[]{:S(2)}) async-start(f32[4,136,256]{2,1,0:T(8,128)} %maximum_bitcast_fusion), calls=%async_computation | async-start | bytes 1114112 | tf_op jit(solution)/shard_map/all_to_all | solution.py:104
  29.4 41.3 %collective-permute-start = (bf16[64,512]{1,0:T(8,128)(2,1)S(1)}, bf16[64,512]{1,0:T(8,128)(2,1)S(1)}, u32[]{:S(2)}, u32[]{:S(2)}) collective-permute-start(bf16[64,512]{1,0:T(8,128)(2,1)S(1)} %copy-done.14), channel_id=1, source_target_pairs={{0,0},{1,4},{2,8},{3,12},{4,1},{5,5},{6,9},{7,13},{8,2},{9,6},{10,... | collective-permute-start | bytes 196616 | tf_op jit(solution)/shard_map/ppermute | solution.py:102
  50.5 20.1 %all-to-all-start.1 = ((f32[4,64,512]{2,1,0:T(8,128)}), f32[4,64,512]{2,1,0:T(8,128)S(1)}, u32[]{:S(2)}, u32[]{:S(2)}) async-start(f32[4,64,512]{2,1,0:T(8,128)} %bitcast.13), calls=%async_computation.1 | async-start | bytes 1048576 | tf_op jit(solution)/shard_map/all_to_all | solution.py:109
  56.2 0.6 copy-start.2
  57.4 55.8 %copy-start.4 = (s32[512,32]{0,1:T(8,128)}, s32[512,32]{0,1:T(8,128)S(1)}, u32[]{:S(2)}) copy-start(s32[512,32]{0,1:T(8,128)S(1)} %reshape.144) | copy-start | bytes 196612
  70.7 42.5 %copy-start.7 = (bf16[64,512]{1,0:T(8,128)(2,1)}, bf16[64,512]{1,0:T(8,128)(2,1)S(1)}, u32[]{:S(2)}) copy-start(bf16[64,512]{1,0:T(8,128)(2,1)S(1)} %collective-permute-done) | copy-start | bytes 196612
  129.2 5.4 %copy-start.3 = (s32[8,64,6]{1,2,0:T(8,128)S(1)}, s32[8,64,6]{1,2,0:T(8,128)}, u32[]{:S(2)}) copy-start(s32[8,64,6]{1,2,0:T(8,128)} %copy-done.2) | copy-start | bytes 36868
  129.2 5.4 %copy-start.9 = (f32[8,64,6]{1,2,0:T(8,128)S(1)}, f32[8,64,6]{1,2,0:T(8,128)}, u32[]{:S(2)}) copy-start(f32[8,64,6]{1,2,0:T(8,128)} %get-tuple-element.13) | copy-start | bytes 36868
  129.3 5.7 %copy-start.15 = (u32[32]{0:T(128)S(1)}, u32[32]{0:T(128)}, u32[]{:S(2)}) copy-start(u32[32]{0:T(128)} %constant.96) | copy-start | bytes 388
  129.3 59.5 %copy-start.5 = (s32[512,32]{0,1:T(8,128)S(1)}, s32[512,32]{0,1:T(8,128)}, u32[]{:S(2)}) copy-start(s32[512,32]{0,1:T(8,128)} %copy-done.4) | copy-start | bytes 196612
  129.3 61.1 %all-to-all-start.2 = ((bf16[4,512,2,352]{1,3,2,0:T(8,128)(2,1)}), bf16[4,512,2,352]{1,3,2,0:T(8,128)(2,1)S(1)}, u32[]{:S(2)}, u32[]{:S(2)}) async-start(bf16[4,512,2,352]{1,3,2,0:T(8,128)(2,1)} %pad_maximum_fusion), calls=%async_computation.2 | async-start | bytes 5767168 | tf_op jit(solution)/shard_map/all_to_all | solution.py:127
  134.6 74.9 %all-gather.4.cloned.1.call-start = ((), (), s32[]{:S(2)}) async-start(), calls=%async_computation.4 | async-start | bytes 1966080 | tf_op jit(solution)/shard_map/all_gather | solution.py:132
  190.8 18.7 %copy-start.6 = (s32[512,32]{0,1:T(8,128)S(1)}, s32[512,32]{0,1:T(8,128)}, u32[]{:S(2)}) copy-start(s32[512,32]{0,1:T(8,128)} %copy-done.4) | copy-start | bytes 196612
  209.5 29.7 %copy-start.8 = (bf16[64,512]{1,0:T(8,128)(2,1)S(1)}, bf16[64,512]{1,0:T(8,128)(2,1)}, u32[]{:S(2)}) copy-start(bf16[64,512]{1,0:T(8,128)(2,1)} %copy-done.7) | copy-start | bytes 196612
  209.5 38.4 %copy-start.1 = (bf16[512,512]{1,0:T(8,128)(2,1)S(1)}, bf16[512,512]{1,0:T(8,128)(2,1)}, u32[]{:S(2)}) copy-start(bf16[512,512]{1,0:T(8,128)(2,1)} %param.21) | copy-start | bytes 1572868
  239.2 8.0 %collective-permute-start.1 = (bf16[64,512]{1,0:T(8,128)(2,1)S(1)}, bf16[64,512]{1,0:T(8,128)(2,1)S(1)}, u32[]{:S(2)}, u32[]{:S(2)}) collective-permute-start(bf16[64,512]{1,0:T(8,128)(2,1)S(1)} %add_convert_fusion), channel_id=1, source_target_pairs={{0,0},{1,4},{2,8},{3,12},{4,1},{5,5},{6,9},{7,13},{8,2},{9,6},{10,... | collective-permute-start | bytes 196616 | tf_op jit(solution)/shard_map/ppermute | solution.py:139
Sparse Core Ops, SparseCore 0:
  192.7 16.7 all-gather.3
where the time goes:
time: 256 us; the launch traced here: 255 us
  blocking collectives  121 us (47%)
  matrix products  38.5 us (15%)
  waiting for transfers between devices  34.6 us (14%)
  starting transfers between devices  21.2 us (8%)
  between operations  14.5 us (6%)
  other arithmetic  14 us (5%)
  local copies, waits for them, and re-layouts  10.6 us (4%)
    psum x1, blocking collectives, body(): squares = lax.psum(squares, 'ctx')  33.5 us
    all_gather x1, blocking collectives, body(): scaled = lax.all_gather(scaled, ('req', 'tp'), tiled=True)  32.5 us
    all_to_all x1, blocking collectives, body(): mixed = lax.all_to_all(mixed, ('req', 'tp'), 0, 0, tiled=True)  21.4 us
    unnamed x1, blocking collectives  18.9 us
    all_gather x1, waiting for transfers between devices, body(): inner = lax.all_gather(inner, 'ctx', tiled=True).reshape(exp_dev, slots, -1)  17 us
    all_to_all x1, waiting for transfers between devices, body(): part = lax.all_to_all(part, 'tp', 0, 0, tiled=True)  12.4 us
    all_gather x1, blocking collectives, route_tables(): both = lax.all_gather(both, ('req', 'ctx'))  9.25 us
    dot_general x1, matrix products, body(): jnp.einsum('esd,edf->esf', rows, w_up, preferred_element_type=jnp.float32)  8.61 us
  transfers between devices with their start and end apart: 6, of which 3 were waited for; matrix products, arithmetic and copies ran while one was open for 2% of the time, Pallas kernels for 0%

commit v1 on v0

--- a/solution.py
+++ b/solution.py
@@ -103,7 +103,12 @@
     packs = attention_part(queries, new_keys, new_values, cache_keys, cache_values, length)
     packs = lax.all_to_all(packs, "ctx", 0, 0, tiled=True)
     attended = merge(packs, hd, heads)
-    attended = lax.all_gather(attended, "ctx", tiled=True)
+    ring = [attended]
+    for hop in range(3):
+        ring.append(lax.ppermute(ring[-1], "ctx", [(dev, (dev + 1) % 4) for dev in range(4)]))
+    attended = jnp.roll(
+        jnp.concatenate(ring[::-1], axis=0), (lax.axis_index("ctx") + 1) * ring[0].shape[0], axis=0
+    )
     part = jnp.dot(attended, out_weight, preferred_element_type=jnp.float32)
     part = part.reshape(-1, block, share)
     part = lax.all_to_all(part, "tp", 0, 0, tiled=True)

time: 256 us -> 259 us (1.012)
  blocking collectives: 121 us -> 126 us
  starting transfers between devices: 21.2 us -> 18.4 us
    all_to_all x0 -> x1, blocking collectives: none -> 10.6 us  [body(): packs = lax.all_to_all(packs, 'ctx', 0, 0, tiled=True)]
    all_gather x1 -> x0, blocking collectives: 5.85 us -> none  [body(): attended = lax.all_gather(attended, 'ctx', tiled=True)]
    all_to_all x1 -> x0, starting transfers between devices: 3.46 us -> none  [body(): packs = lax.all_to_all(packs, 'ctx', 0, 0, tiled=True)]
    ppermute x0 -> x3, waiting for transfers between devices: none -> 3.32 us  [body(): lax.ppermute(ring[-1], 'ctx', [(dev, (dev + 1) % 4) for dev in range(4)])]
  transfers between devices with their start and end apart: 6 -> 8, of which waited for: 3 -> 4; matrix products, arithmetic and copies ran while one was open for 2% -> 2% of each run, Pallas kernels for 0% -> 0%
where the time goes in v1:
time: 259 us; the launch traced here: 258 us
  blocking collectives  126 us (49%)
  matrix products  38.5 us (15%)
  waiting for transfers between devices  36.3 us (14%)
  starting transfers between devices  18.4 us (7%)
  between operations  14.6 us (6%)
  other arithmetic  13.4 us (5%)
  local copies, waits for them, and re-layouts  10.7 us (4%)
    psum x1, blocking collectives, body(): squares = lax.psum(squares, 'ctx')  33.5 us
    all_gather x1, blocking collectives, body(): scaled = lax.all_gather(scaled, ('req', 'tp'), tiled=True)  32.6 us
    all_to_all x1, blocking collectives, body(): mixed = lax.all_to_all(mixed, ('req', 'tp'), 0, 0, tiled=True)  21.4 us
    unnamed x1, blocking collectives  19.1 us
    all_gather x1, waiting for transfers between devices, body(): inner = lax.all_gather(inner, 'ctx', tiled=True).reshape(exp_dev, slots, -1)  17.1 us
    all_to_all x1, blocking collectives, body(): packs = lax.all_to_all(packs, 'ctx', 0, 0, tiled=True)  10.6 us
    all_to_all x1, waiting for transfers between devices, body(): part = lax.all_to_all(part, 'tp', 0, 0, tiled=True)  10.6 us
    all_gather x1, blocking collectives, route_tables(): both = lax.all_gather(both, ('req', 'ctx'))  9.21 us
  transfers between devices with their start and end apart: 8, of which 4 were waited for; matrix products, arithmetic and copies ran while one was open for 2% of the time, Pallas kernels for 0%

profile of v1, /device:TPU:4, one launch (start us, length us, event | category | flops | bytes accessed | tf_op | source)
XLA Modules:
  0.0 258.4 jit_solution(1240053992585343936)
XLA Ops:
  6.6 1.0 copy.55
  7.6 1.2 dynamic_slice.14
  8.9 0.7 add_compare_fusion
  9.5 6.5 %fusion = (f32[1024]{0:T(1024)S(1)}, f32[2304,1024]{1,0:T(8,128)S(1)}) fusion(s32[1024]{0:T(1024)S(1)} %fusion.40, s32[2304]{0:T(1024)S(1)} %iota_add_fusion, pred[2304]{0:T(1024)(128)(4,1)S(1)} %get-tuple-element.17, pred[2304]{0:T(1024)(128)(4,1)S(1)} %get-tuple-element.18, pred[]{:T(512)S(6)} %eq.34, bf16[1024,128]{1,0:T(8,128)(2,1)S(1)} %bitcast.90, ...), kind=kOutput, calls=%fused_computation.3 | convolution fusion | flops 619314176 | bytes 10311169 | tf_op jit(solution)/shard_map/dot_general | solution.py:21
  16.0 4.7 %fusion.1 = f32[1024]{0:T(1024)S(1)} fusion(f32[2304,1024]{1,0:T(8,128)S(1)} %get-tuple-element.16, f32[1024]{0:T(1024)S(1)} %get-tuple-element.15, s32[1024]{0:T(1024)S(1)} %fusion.40, s32[2304]{0:T(1024)S(1)} %iota_add_fusion, pred[2304]{0:T(1024)(128)(4,1)S(1)} %get-tuple-element.17, pred[2304]{0:T(1024)(128)(4,1)S(1)} %get-tuple-element.18, pred[]{:T(512)S(6)} %eq.34), kind=kLoop, calls=%fused_computation.5 | loop fusion | flops 18873344 | bytes 9463297 | tf_op jit(solution)/shard_map/reduce_sum | solution.py:33
  20.8 4.0 %fusion.3 = f32[128,1024]{1,0:T(8,128)S(1)} fusion(f32[2304,1024]{1,0:T(8,128)S(1)} %get-tuple-element.16, f32[1024]{0:T(1024)S(1)} %get-tuple-element.15, s32[1024]{0:T(1024)S(1)} %fusion.40, s32[2304]{0:T(1024)S(1)} %iota_add_fusion, pred[2304]{0:T(1024)(128)(4,1)S(1)} %get-tuple-element.17, pred[2304]{0:T(1024)(128)(4,1)S(1)} %get-tuple-element.18, ...), kind=kOutput, calls=%fused_computation.7 | convolution fusion | flops 624033792 | bytes 10573313 | tf_op jit(solution)/shard_map/dot_general | solution.py:34
  25.1 10.6 %all_to_all.20 = f32[4,136,256]{2,1,0:T(8,128)S(1)} all-to-all(f32[4,136,256]{2,1,0:T(8,128)S(1)} %maximum_bitcast_fusion), channel_id=1, replica_groups=mesh['req'=2,'ctx'=4,'tp'=4] {'ctx'}, dimensions={0} | all-to-all | bytes 1114112 | tf_op jit(solution)/shard_map/all_to_all | solution.py:104
  36.2 5.6 %collective-permute-start.3 = (bf16[64,512]{1,0:T(8,128)(2,1)S(1)}, bf16[64,512]{1,0:T(8,128)(2,1)S(1)}, u32[]{:S(2)}, u32[]{:S(2)}) collective-permute-start(bf16[64,512]{1,0:T(8,128)(2,1)S(1)} %copy-done.14), channel_id=1, source_target_pairs={{0,0},{1,4},{2,8},{3,12},{4,1},{5,5},{6,9},{7,13},{8,2},{9,6},{10,... | collective-permute-start | bytes 196616 | tf_op jit(solution)/shard_map/ppermute | solution.py:102
  41.9 1.2 collective-permute-start.1
  43.1 9.2 %all-gather.1 = f32[8,64,12]{1,2,0:T(8,128)S(1)} all-gather(f32[1,64,12]{1,2,0:T(8,128)S(1)} %maximum_bitcast_fusion.1), channel_id=2, replica_groups=mesh['req'=2,'ctx'=4,'tp'=4] {'req','ctx'}, dimensions={0}, use_global_device_ids=true | all-gather | bytes 27648 | tf_op jit(solution)/shard_map/all_gather | solution.py:56
  52.7 3.3 %collective-permute-done.2 = bf16[64,512]{1,0:T(8,128)(2,1)S(1)} collective-permute-done((bf16[64,512]{1,0:T(8,128)(2,1)S(1)}, bf16[64,512]{1,0:T(8,128)(2,1)S(1)}, u32[]{:S(2)}, u32[]{:S(2)}) %collective-permute-start.2) | collective-permute-done | bytes 65568 | tf_op jit(solution)/shard_map/ppermute | solution.py:108
  56.3 1.1 fusion.26
  57.4 3.5 %all-to-all-start.1 = ((f32[4,64,512]{2,1,0:T(8,128)}), f32[4,64,512]{2,1,0:T(8,128)S(1)}, u32[]{:S(2)}, u32[]{:S(2)}) async-start(f32[4,64,512]{2,1,0:T(8,128)} %bitcast.13), calls=%async_computation.1 | async-start | bytes 1048576 | tf_op jit(solution)/shard_map/all_to_all | solution.py:114
  62.7 0.8 dynamic_slice.16
  63.5 10.6 %all-to-all-done.1 = f32[4,64,512]{2,1,0:T(8,128)S(1)} async-done(((f32[4,64,512]{2,1,0:T(8,128)}), f32[4,64,512]{2,1,0:T(8,128)S(1)}, u32[]{:S(2)}, u32[]{:S(2)}) %all-to-all-start.1) | async-done | bytes 524320 | tf_op jit(solution)/shard_map/all_to_all | solution.py:114
  74.2 32.6 %all_gather.17 = bf16[512,512]{1,0:T(8,128)(2,1)S(1)} all-gather(bf16[64,512]{1,0:T(8,128)(2,1)S(1)} %get-tuple-element.12), channel_id=1, replica_groups=mesh['req'=2,'ctx'=4,'tp'=4] {'req','tp'}, dimensions={0}, use_global_device_ids=true | all-gather | bytes 589824 | tf_op jit(solution)/shard_map/all_gather | solution.py:122
  106.9 1.3 fusion.6
  108.1 8.6 %convolution_convert_fusion = bf16[32,64,352]{2,1,0:T(8,128)(2,1)} fusion(bf16[32,64,512]{2,1,0:T(8,128)(2,1)S(1)} %fusion.6, bf16[32,512,352]{1,2,0:T(8,128)(2,1)} %param.26), kind=kOutput, calls=%fused_computation.17 | convolution fusion | flops 738918400 | bytes 15073280 | tf_op jit(solution)/shard_map/esd,edf->esf/dot_general | solution.py:129
  116.7 2.5 copy.63
  119.3 8.6 %convolution_convert_fusion.1 = bf16[32,64,352]{2,1,0:T(8,128)(2,1)} fusion(bf16[32,64,512]{2,1,0:T(8,128)(2,1)S(1)} %fusion.6, bf16[32,512,352]{1,2,0:T(8,128)(2,1)} %param.25), kind=kOutput, calls=%fused_computation.18 | convolution fusion | flops 738918400 | bytes 15073280 | tf_op jit(solution)/shard_map/esd,edf->esf/dot_general | solution.py:128
  127.9 1.7 copy.62
  129.6 3.2 %pad_maximum_fusion = bf16[4,512,2,352]{1,3,2,0:T(8,128)(2,1)} fusion(bf16[4,512,1,352]{1,3,2,0:T(8,128)(2,1)} %copy.63, bf16[4,512,1,352]{1,3,2,0:T(8,128)(2,1)S(1)} %copy.62), kind=kLoop, calls=%fused_computation.14 | loop fusion | flops 1441792 | bytes 5767168 | tf_op jit(solution)/shard_map/stack | solution.py:130
  132.8 5.0 %all-to-all-start.2 = ((bf16[4,512,2,352]{1,3,2,0:T(8,128)(2,1)}), bf16[4,512,2,352]{1,3,2,0:T(8,128)(2,1)S(1)}, u32[]{:S(2)}, u32[]{:S(2)}) async-start(bf16[4,512,2,352]{1,3,2,0:T(8,128)(2,1)} %pad_maximum_fusion), calls=%async_computation.2 | async-start | bytes 5767168 | tf_op jit(solution)/shard_map/all_to_all | solution.py:132
  139.5 33.5 %psum.7 = f32[64]{0:T(128)S(1)} all-reduce(f32[64]{0:T(128)S(1)} %get-tuple-element.11), channel_id=1, replica_groups=mesh['req'=2,'ctx'=4,'tp'=4] {'ctx'}, use_global_device_ids=true, to_apply=%region_9.10 | all-reduce | flops 64 | bytes 512 | tf_op jit(solution)/shard_map/psum | solution.py:119
  173.1 19.1 %all-reduce = f32[512]{0:T(512)S(1)} all-reduce(f32[512]{0:T(512)S(1)} %rsqrt_dynamic-update-slice_fusion), channel_id=1, replica_groups=mesh['req'=2,'ctx'=4,'tp'=4] {'req','tp'}, use_global_device_ids=true, to_apply=%add | all-reduce | flops 512 | bytes 4096
  192.3 1.5 select_reduce_fusion
  195.0 1.0 fusion.16
  196.0 17.1 %all-gather.4.cloned.1.call-done = bf16[2048,352]{1,0:T(8,128)(2,1)} async-done(((bf16[512,352]{1,0:T(8,128)(2,1)}), bf16[2048,352]{1,0:T(8,128)(2,1)}) %all-gather.4.cloned.1.call-update) | async-done | bytes 1441808 | tf_op jit(solution)/shard_map/all_gather | solution.py:137
  213.2 8.2 %fusion.10 = bf16[512,512]{1,0:T(8,128)(2,1)S(1)} fusion(s32[32,512]{1,0:T(8,128)S(1)} %bitcast.93, bf16[32,64,352]{2,1,0:T(8,128)(2,1)} %bitcast.99, bf16[32,352,512]{2,1,0:T(8,128)(2,1)} %param.27, f32[32,64]{1,0:T(8,128)S(1)} %get-tuple-element.5), kind=kOutput, calls=%fused_computation.20 | convolution fusion | flops 1815347200 | bytes 13574144 | tf_op jit(solution)/shard_map/est,esd->td/dot_general | solution.py:140
  221.4 21.4 %all_to_all.21 = bf16[8,64,512]{2,1,0:T(8,128)(2,1)S(1)} all-to-all(bf16[8,64,512]{2,1,0:T(8,128)(2,1)S(1)} %bitcast.89), channel_id=1, replica_groups=mesh['req'=2,'ctx'=4,'tp'=4] {'req','tp'}, dimensions={0} | all-to-all | bytes 1048576 | tf_op jit(solution)/shard_map/all_to_all | solution.py:142
  242.9 2.7 %collective-permute-start.4 = (bf16[64,512]{1,0:T(8,128)(2,1)S(1)}, bf16[64,512]{1,0:T(8,128)(2,1)S(1)}, u32[]{:S(2)}, u32[]{:S(2)}) collective-permute-start(bf16[64,512]{1,0:T(8,128)(2,1)S(1)} %add_convert_fusion), channel_id=1, source_target_pairs={{0,0},{1,4},{2,8},{3,12},{4,1},{5,5},{6,9},{7,13},{8,2},{9,6},{10,... | collective-permute-start | bytes 196616 | tf_op jit(solution)/shard_map/ppermute | solution.py:144
  245.6 5.3 %collective-permute-done.4 = bf16[64,512]{1,0:T(8,128)(2,1)S(1)} collective-permute-done((bf16[64,512]{1,0:T(8,128)(2,1)S(1)}, bf16[64,512]{1,0:T(8,128)(2,1)S(1)}, u32[]{:S(2)}, u32[]{:S(2)}) %collective-permute-start.4) | collective-permute-done | bytes 65568 | tf_op jit(solution)/shard_map/ppermute | solution.py:144
  (89 shorter events, 6.4 us)
Async XLA Ops:
  6.5 49.7 %copy-start = (bf16[512,512]{1,0:T(8,128)(2,1)S(1)}, bf16[512,512]{1,0:T(8,128)(2,1)}, u32[]{:S(2)}) copy-start(bf16[512,512]{1,0:T(8,128)(2,1)} %param.21) | copy-start | bytes 1572868
  16.0 4.8 %copy-start.12 = (bf16[1,2048,1,128]{3,1,2,0:T(8,128)(2,1)S(1)}, bf16[1,2048,1,128]{3,1,2,0:T(8,128)(2,1)}, u32[]{:S(2)}) copy-start(bf16[1,2048,1,128]{3,1,2,0:T(8,128)(2,1)} %param.18) | copy-start | bytes 1572868
  16.0 4.8 %copy-start.13 = (bf16[256,1,128]{2,0,1:T(8,128)(2,1)S(1)}, bf16[256,1,128]{2,0,1:T(8,128)(2,1)}, u32[]{:S(2)}) copy-start(bf16[256,1,128]{2,0,1:T(8,128)(2,1)} %param.16) | copy-start | bytes 196612
  24.8 11.4 %copy-start.14 = (bf16[64,512]{1,0:T(8,128)(2,1)S(1)}, bf16[64,512]{1,0:T(8,128)(2,1)}, u32[]{:S(2)}) copy-start(bf16[64,512]{1,0:T(8,128)(2,1)} %param.20) | copy-start | bytes 196612
  24.8 17.0 %copy-start.10 = (s32[64,6]{0,1:T(8,128)S(1)}, s32[64,6]{0,1:T(8,128)}, u32[]{:S(2)}) copy-start(s32[64,6]{0,1:T(8,128)} %param.23) | copy-start | bytes 4612
  24.8 18.2 %copy-start.11 = (f32[64,6]{0,1:T(8,128)S(1)}, f32[64,6]{0,1:T(8,128)}, u32[]{:S(2)}) copy-start(f32[64,6]{0,1:T(8,128)} %param.24) | copy-start | bytes 4612
  36.1 5.7 %collective-permute-start = (bf16[64,512]{1,0:T(8,128)(2,1)S(1)}, bf16[64,512]{1,0:T(8,128)(2,1)S(1)}, u32[]{:S(2)}, u32[]{:S(2)}) collective-permute-start(bf16[64,512]{1,0:T(8,128)(2,1)S(1)} %copy_bitcast_fusion.1), channel_id=1, source_target_pairs={{0,4},{4,8},{8,12},{12,0},{1,5},{5,9},{9,13},{13,1},{2,6},{6,10},{... | collective-permute-start | bytes 196616 | tf_op jit(solution)/shard_map/ppermute | solution.py:108
  36.2 37.9 %collective-permute-start.3 = (bf16[64,512]{1,0:T(8,128)(2,1)S(1)}, bf16[64,512]{1,0:T(8,128)(2,1)S(1)}, u32[]{:S(2)}, u32[]{:S(2)}) collective-permute-start(bf16[64,512]{1,0:T(8,128)(2,1)S(1)} %copy-done.14), channel_id=1, source_target_pairs={{0,0},{1,4},{2,8},{3,12},{4,1},{5,5},{6,9},{7,13},{8,2},{9,6},{10,... | collective-permute-start | bytes 196616 | tf_op jit(solution)/shard_map/ppermute | solution.py:102
  41.9 10.4 %collective-permute-start.1 = (bf16[64,512]{1,0:T(8,128)(2,1)S(1)}, bf16[64,512]{1,0:T(8,128)(2,1)S(1)}, u32[]{:S(2)}, u32[]{:S(2)}) collective-permute-start(bf16[64,512]{1,0:T(8,128)(2,1)S(1)} %collective-permute-done), channel_id=1, source_target_pairs={{0,4},{4,8},{8,12},{12,0},{1,5},{5,9},{9,13},{13,1},{2,6},{6,10},{... | collective-permute-start | bytes 196616 | tf_op jit(solution)/shard_map/ppermute | solution.py:108
  52.3 3.7 %collective-permute-start.2 = (bf16[64,512]{1,0:T(8,128)(2,1)S(1)}, bf16[64,512]{1,0:T(8,128)(2,1)S(1)}, u32[]{:S(2)}, u32[]{:S(2)}) collective-permute-start(bf16[64,512]{1,0:T(8,128)(2,1)S(1)} %collective-permute-done.1), channel_id=1, source_target_pairs={{0,4},{4,8},{8,12},{12,0},{1,5},{5,9},{9,13},{13,1},{2,6},{6,10},{... | collective-permute-start | bytes 196616 | tf_op jit(solution)/shard_map/ppermute | solution.py:108
  57.4 16.7 %all-to-all-start.1 = ((f32[4,64,512]{2,1,0:T(8,128)}), f32[4,64,512]{2,1,0:T(8,128)S(1)}, u32[]{:S(2)}, u32[]{:S(2)}) async-start(f32[4,64,512]{2,1,0:T(8,128)} %bitcast.13), calls=%async_computation.1 | async-start | bytes 1048576 | tf_op jit(solution)/shard_map/all_to_all | solution.py:114
  61.5 0.6 copy-start.2
  62.7 54.1 %copy-start.4 = (s32[512,32]{0,1:T(8,128)}, s32[512,32]{0,1:T(8,128)S(1)}, u32[]{:S(2)}) copy-start(s32[512,32]{0,1:T(8,128)S(1)} %reshape.144) | copy-start | bytes 196612
  74.1 42.6 %copy-start.7 = (bf16[64,512]{1,0:T(8,128)(2,1)}, bf16[64,512]{1,0:T(8,128)(2,1)S(1)}, u32[]{:S(2)}) copy-start(bf16[64,512]{1,0:T(8,128)(2,1)S(1)} %collective-permute-done.3) | copy-start | bytes 196612
  132.8 5.0 %copy-start.3 = (s32[8,64,6]{1,2,0:T(8,128)S(1)}, s32[8,64,6]{1,2,0:T(8,128)}, u32[]{:S(2)}) copy-start(s32[8,64,6]{1,2,0:T(8,128)} %copy-done.2) | copy-start | bytes 36868
  132.8 5.0 %copy-start.9 = (f32[8,64,6]{1,2,0:T(8,128)S(1)}, f32[8,64,6]{1,2,0:T(8,128)}, u32[]{:S(2)}) copy-start(f32[8,64,6]{1,2,0:T(8,128)} %get-tuple-element.13) | copy-start | bytes 36868
  132.8 5.4 %copy-start.15 = (u32[32]{0:T(128)S(1)}, u32[32]{0:T(128)}, u32[]{:S(2)}) copy-start(u32[32]{0:T(128)} %constant.117) | copy-start | bytes 388
  132.8 59.4 %copy-start.5 = (s32[512,32]{0,1:T(8,128)S(1)}, s32[512,32]{0,1:T(8,128)}, u32[]{:S(2)}) copy-start(s32[512,32]{0,1:T(8,128)} %copy-done.4) | copy-start | bytes 196612
  132.8 61.0 %all-to-all-start.2 = ((bf16[4,512,2,352]{1,3,2,0:T(8,128)(2,1)}), bf16[4,512,2,352]{1,3,2,0:T(8,128)(2,1)S(1)}, u32[]{:S(2)}, u32[]{:S(2)}) async-start(bf16[4,512,2,352]{1,3,2,0:T(8,128)(2,1)} %pad_maximum_fusion), calls=%async_computation.2 | async-start | bytes 5767168 | tf_op jit(solution)/shard_map/all_to_all | solution.py:132
  137.8 75.3 %all-gather.4.cloned.1.call-start = ((), (), s32[]{:S(2)}) async-start(), calls=%async_computation.4 | async-start | bytes 1966080 | tf_op jit(solution)/shard_map/all_gather | solution.py:137
  194.3 18.8 %copy-start.6 = (s32[512,32]{0,1:T(8,128)S(1)}, s32[512,32]{0,1:T(8,128)}, u32[]{:S(2)}) copy-start(s32[512,32]{0,1:T(8,128)} %copy-done.4) | copy-start | bytes 196612
  213.1 29.7 %copy-start.8 = (bf16[64,512]{1,0:T(8,128)(2,1)S(1)}, bf16[64,512]{1,0:T(8,128)(2,1)}, u32[]{:S(2)}) copy-start(bf16[64,512]{1,0:T(8,128)(2,1)} %copy-done.7) | copy-start | bytes 196612
  213.1 38.4 %copy-start.1 = (bf16[512,512]{1,0:T(8,128)(2,1)S(1)}, bf16[512,512]{1,0:T(8,128)(2,1)}, u32[]{:S(2)}) copy-start(bf16[512,512]{1,0:T(8,128)(2,1)} %param.21) | copy-start | bytes 1572868
  242.9 8.0 %collective-permute-start.4 = (bf16[64,512]{1,0:T(8,128)(2,1)S(1)}, bf16[64,512]{1,0:T(8,128)(2,1)S(1)}, u32[]{:S(2)}, u32[]{:S(2)}) collective-permute-start(bf16[64,512]{1,0:T(8,128)(2,1)S(1)} %add_convert_fusion), channel_id=1, source_target_pairs={{0,0},{1,4},{2,8},{3,12},{4,1},{5,5},{6,9},{7,13},{8,2},{9,6},{10,... | collective-permute-start | bytes 196616 | tf_op jit(solution)/shard_map/ppermute | solution.py:144
Sparse Core Ops, SparseCore 0:
  196.2 16.9 all-gather.3
